TPU v7x, 32 devices: a whole 2x2x4 slice. The times are simulated.
32 devices in a mesh: seq: 8 (over y, x, core), head: 4 (over z).
Axes of the slice: x: 2, y: 2, z: 4, core: 2. Of those that a mesh axis runs over, the one named last changes fastest.
Arguments:
- query_lin: bfloat16 [512, 4096], P('seq', 'head'), may hold values from -6 to 6
- key_lin: bfloat16 [512, 4096], P('seq', 'head'), may hold values from -6 to 6
- value_lin: bfloat16 [512, 4096], P('seq', 'head'), may hold values from -6 to 6
- log_decay: float32 [32, 512], P('head', 'seq'), may hold values from -1.6 to 0
- query_soft: bfloat16 [512, 4096], P(('seq', 'head')), may hold values from -4.5 to 4.5
- key_soft: bfloat16 [512, 512], P(('seq', 'head')), may hold values from -4.5 to 4.5
- value_soft: bfloat16 [512, 512], P(('seq', 'head')), may hold values from -6 to 6
- doc_start: int32 [512], P('seq'), may hold values from 0 to 480, as said below
Outputs:
- lin_out: bfloat16 [512, 4096], P('seq', 'head')
- soft_out: bfloat16 [512, 4096], P('seq', 'head')
- soft_lse: float32 [32, 512], P('head', 'seq')
Inputs may be any that keep to these rules, and one draw needn't show every extreme that they name: doc_start[t] is the first position of the document that holds token t: 0 for the first document, never above t, the same over a document; at most 4 documents; every document but the first and the last starts at a position of 1 to 32; the last document starts at 480.
All inputs are finite; a program needn't handle non-finite values.
Results may differ from a plain program's by a relative error of at most 0.003.
Values may be sent and summed in bfloat16 or wider, within the bound.
A program may use at most 256 MiB of HBM per device.

v0:
```python
import jax
import jax.numpy as jnp
from jax import lax
from jax.sharding import PartitionSpec as P

DH = 128
HIGHEST = lax.Precision.HIGHEST
masked_score = -1e30


def prefix(array, axis, combine, identity):
    size, here = (lax.axis_size(axis), lax.axis_index(axis))
    everything = jax.tree.map(lambda part: lax.all_gather(part, axis), array)
    start = jax.tree.map(
        lambda part, zero: jnp.broadcast_to(jnp.asarray(zero, part.dtype), part.shape),
        array,
        identity,
    )

    def lap(k, before):
        reached = k < here
        new = combine(before, jax.tree.map(lambda part: part[k], everything))
        return jax.tree.map(lambda a, b: jnp.where(reached, a, b), new, before)

    return lax.fori_loop(0, size, lap, start)


def span_terms(query_heads, key_heads, value_heads, decay_rows, doc_rows, first_place):
    span_len = query_heads.shape[0]
    cumulative = jnp.cumsum(decay_rows, axis=1)
    totals = cumulative[:, -1]
    token_positions = first_place + jnp.arange(span_len, dtype=jnp.int32)
    allowed = (token_positions[None, :] <= token_positions[:, None]) & (
        doc_rows[:, None] <= token_positions[None, :]
    )
    decay_gap = jnp.where(allowed[None], cumulative[:, :, None] - cumulative[:, None, :], 0.0)
    decay_mat = jnp.where(allowed[None], jnp.exp(decay_gap), 0.0)
    scores = jnp.einsum("thd,shd->hts", query_heads, key_heads, preferred_element_type=jnp.float32)
    key_float = key_heads.astype(jnp.float32)
    value_float = value_heads.astype(jnp.float32)
    inner_part = jnp.einsum("hts,shd->thd", scores * decay_mat, value_float, precision=HIGHEST)
    keep_mask = (doc_rows == doc_rows[-1]).astype(jnp.float32)
    tail_weight = jnp.exp(totals[:, None] - cumulative) * keep_mask[None, :]
    weighted_keys = key_float * jnp.transpose(tail_weight)[:, :, None]
    fresh_state = jnp.einsum("shd,she->hde", weighted_keys, value_float, precision=HIGHEST)
    carry_on = (doc_rows[-1] < first_place).astype(jnp.float32)
    factor = jnp.exp(totals) * carry_on
    read_mask = (doc_rows < first_place).astype(jnp.float32)[:, None] * jnp.transpose(
        jnp.exp(cumulative)
    )
    return (inner_part, fresh_state, factor, read_mask)


def combine_states(earlier, later_part):
    return (earlier[0] * later_part[0], later_part[0][:, None, None] * earlier[1] + later_part[1])


def lightning_part(query_lin, key_lin, value_lin, log_decay, doc_start):
    span_len = query_lin.shape[0]
    head_count = log_decay.shape[0]
    first_place = lax.axis_index("seq") * span_len
    query_heads = query_lin.reshape(span_len, head_count, DH)
    key_heads = key_lin.reshape(span_len, head_count, DH)
    value_heads = value_lin.reshape(span_len, head_count, DH)
    inner_part, fresh_state, factor, read_mask = span_terms(
        query_heads, key_heads, value_heads, log_decay, doc_start, first_place
    )
    identity = (jnp.ones((head_count,), jnp.float32), jnp.zeros((head_count, DH, DH), jnp.float32))
    unused, carried = prefix((factor, fresh_state), "seq", combine_states, identity)
    outer_part = (
        jnp.einsum("thd,hde->the", query_heads.astype(jnp.float32), carried, precision=HIGHEST)
        * read_mask[:, :, None]
    )
    mixed_out = inner_part + outer_part
    normed = mixed_out * lax.rsqrt(jnp.mean(mixed_out * mixed_out, axis=-1, keepdims=True) + 1e-06)
    return normed.astype(jnp.bfloat16).reshape(span_len, head_count * DH)


def softmax_part(query_soft, key_soft, value_soft, doc_start):
    queries, keys_local, values_local = (
        lax.all_to_all(query_soft, "head", split_axis=1, concat_axis=0, tiled=True),
        lax.all_to_all(key_soft, "head", split_axis=1, concat_axis=0, tiled=True),
        lax.all_to_all(value_soft, "head", split_axis=1, concat_axis=0, tiled=True),
    )
    span_len = queries.shape[0]
    kv_count = keys_local.shape[1] // DH
    group_size = queries.shape[1] // keys_local.shape[1]
    first_place = lax.axis_index("seq") * span_len
    query_places = first_place + jnp.arange(span_len, dtype=jnp.int32)
    query_heads = queries.reshape(span_len, kv_count, group_size, DH)
    score_scale = DH ** (-0.5)
    start_state = (
        jnp.full((span_len, kv_count, group_size), masked_score, jnp.float32),
        jnp.zeros((span_len, kv_count, group_size), jnp.float32),
        jnp.zeros((span_len, kv_count, group_size, DH), jnp.float32),
    )
    key_piece = lax.all_gather(keys_local, "seq", axis=0, tiled=True)
    value_piece = lax.all_gather(values_local, "seq", axis=0, tiled=True)
    piece_rows = key_piece.shape[0]
    block_rows = max(
        (divisor for divisor in range(1, min(piece_rows, 1024) + 1) if piece_rows % divisor == 0)
    )
    block_count = piece_rows // block_rows
    key_parts = key_piece.reshape(block_count, block_rows, kv_count, DH)
    value_parts = value_piece.reshape(block_count, block_rows, kv_count, DH)
    begin_rows = jnp.int32(0) + block_rows * jnp.arange(block_count, dtype=jnp.int32)

    def absorb_block(running, slices):
        key_block, value_block, begin_row = slices
        running_max, norm_sum, accum_out = running
        token_positions = begin_row + jnp.arange(block_rows, dtype=jnp.int32)
        allowed = (token_positions[None, :] <= query_places[:, None]) & (
            doc_start[:, None] <= token_positions[None, :]
        )
        allowed = allowed[:, None, None, :]
        scores = (
            jnp.einsum("tkgd,skd->tkgs", query_heads, key_block, preferred_element_type=jnp.float32)
            * score_scale
        )
        new_max = jnp.maximum(
            running_max, jnp.max(jnp.where(allowed, scores, masked_score), axis=-1)
        )
        raw_weight = jnp.where(allowed, jnp.exp(scores - new_max[..., None]), 0.0)
        shrink = jnp.exp(running_max - new_max)
        norm_sum = norm_sum * shrink + jnp.sum(raw_weight, axis=-1)
        accum_out = accum_out * shrink[..., None] + jnp.einsum(
            "tkgs,skd->tkgd",
            raw_weight.astype(jnp.bfloat16),
            value_block,
            preferred_element_type=jnp.float32,
        )
        running = (new_max, norm_sum, accum_out)
        return (running, None)

    final_state, unused = lax.scan(absorb_block, start_state, (key_parts, value_parts, begin_rows))
    running_max, norm_sum, accum_out = final_state
    soft_out = (
        (accum_out / norm_sum[..., None])
        .astype(jnp.bfloat16)
        .reshape(span_len, kv_count * group_size * DH)
    )
    soft_lse = jnp.transpose(
        (running_max + jnp.log(norm_sum)).reshape(span_len, kv_count * group_size)
    )
    return (soft_out, soft_lse)


def per_device(
    query_lin, key_lin, value_lin, log_decay, query_soft, key_soft, value_soft, doc_start
):
    lin_out = lightning_part(query_lin, key_lin, value_lin, log_decay, doc_start)
    soft_out, soft_lse = softmax_part(query_soft, key_soft, value_soft, doc_start)
    return (lin_out, soft_out, soft_lse)


def solution(mesh):
    return jax.shard_map(
        per_device,
        mesh=mesh,
        in_specs=(
            P("seq", "head"),
            P("seq", "head"),
            P("seq", "head"),
            P("head", "seq"),
            P(("seq", "head"), None),
            P(("seq", "head"), None),
            P(("seq", "head"), None),
            P("seq"),
        ),
        out_specs=(P("seq", "head"), P("seq", "head"), P("head", "seq")),
        check_vma=False,
    )
```

profile of v0, /device:TPU:0, one launch (start us, length us, event | category | flops | bytes accessed | tf_op | source)
XLA Modules:
  0.0 91.8 jit_solution(14963114871208304785)
XLA Ops:
  7.2 0.0 copy-start
  7.2 0.0 all-gather.4.cloned.1.call-start
  7.2 1.2 %slice.8 = s32[1]{0:T(128)} slice(s32[64]{0:T(128)} %param.17), slice={[63:64]} | slice | bytes 8 | tf_op jit(solution)/shard_map/slice | solution.py:46
  9.1 1.3 %compare_convert_fusion = (f32[64]{0:T(128)S(1)}, f32[64]{0:T(128)S(1)}) fusion(s32[64]{0:T(128)} %param.17, s32[]{:T(128)S(6)} %mul.138, s32[]{:T(128)} %bitcast.1), kind=kLoop, calls=%fused_computation.64 | loop fusion | flops 256 | bytes 776 | tf_op jit(solution)/shard_map/convert_element_type | solution.py:48
  10.4 0.9 reduce_window_sum.11
  11.3 0.2 slice_reduce_fusion
  11.5 0.1 multiply_bitcast_fusion
  11.6 0.0 copy-done
  11.6 2.4 %fusion.11 = f32[8,128,128]{2,1,0:T(8,128)} fusion(f32[64,8]{0,1:T(8,128)S(1)} %get-tuple-element.160, bf16[64,1024]{1,0:T(8,128)(2,1)S(1)} %copy-done, bf16[64,1024]{1,0:T(8,128)(2,1)} %param.11), kind=kOutput, calls=%fused_computation.22 | convolution fusion | flops 100794368 | bytes 788480 | tf_op jit(solution)/shard_map/shd,she->hde/dot_general | solution.py:45
  14.0 0.0 all-gather.4.cloned.1.call-update
  14.0 1.3 %copy_bitcast_fusion.4 = bf16[16,4,128]{2,0,1:T(8,128)(2,1)} fusion(bf16[16,512]{1,0:T(8,128)(2,1)} %param.15), kind=kLoop, calls=%fused_computation.50 | loop fusion | bytes 32768 | tf_op jit(solution)/shard_map/all_to_all | solution.py:82
  15.3 6.3 %all-to-all-start = ((bf16[16,4,128]{2,0,1:T(8,128)(2,1)}), bf16[16,4,128]{2,0,1:T(8,128)(2,1)S(1)}, u32[]{:S(2)}, u32[]{:S(2)}) async-start(bf16[16,4,128]{2,0,1:T(8,128)(2,1)} %copy_bitcast_fusion.4), calls=%async_computation | async-start | bytes 32768 | tf_op jit(solution)/shard_map/all_to_all | solution.py:82
  21.7 1.3 %copy_bitcast_fusion.3 = bf16[16,4,128]{2,0,1:T(8,128)(2,1)} fusion(bf16[16,512]{1,0:T(8,128)(2,1)} %param.16), kind=kLoop, calls=%fused_computation.49 | loop fusion | bytes 32768 | tf_op jit(solution)/shard_map/all_to_all | solution.py:83
  23.0 0.7 compare_and_fusion
  23.7 3.5 %all-to-all-done = bf16[16,4,128]{2,0,1:T(8,128)(2,1)S(1)} async-done(((bf16[16,4,128]{2,0,1:T(8,128)(2,1)}), bf16[16,4,128]{2,0,1:T(8,128)(2,1)S(1)}, u32[]{:S(2)}, u32[]{:S(2)}) %all-to-all-start) | async-done | bytes 16416 | tf_op jit(solution)/shard_map/all_to_all | solution.py:82
  27.3 3.3 %all-to-all-start.2 = ((bf16[16,4,128]{2,0,1:T(8,128)(2,1)}), bf16[16,4,128]{2,0,1:T(8,128)(2,1)S(1)}, u32[]{:S(2)}, u32[]{:S(2)}) async-start(bf16[16,4,128]{2,0,1:T(8,128)(2,1)} %copy_bitcast_fusion.3), calls=%async_computation.2 | async-start | bytes 32768 | tf_op jit(solution)/shard_map/all_to_all | solution.py:83
  30.5 1.2 %convolution_multiply_fusion.1 = f32[8,64,64]{2,1,0:T(8,128)S(1)} fusion(f32[8,64]{1,0:T(8,128)S(1)} %reduce_window_sum.11, pred[64,64]{1,0:T(8,128)(4,1)S(1)} %compare_and_fusion, bf16[64,1024]{1,0:T(8,128)(2,1)} %param.11, bf16[64,1024]{1,0:T(8,128)(2,1)} %param.10), kind=kOutput, calls=%fused_computation.10 | convolution fusion | flops 8519680 | bytes 399360 | tf_op jit(solution)/shard_map/thd,shd->hts/dot_general | solution.py:38
  31.7 1.2 %dynamic-slice = u32[1]{0:T(128)} dynamic-slice(u32[32]{0:T(128)} %constant.72, u32[]{:T(128)S(6)} %add.102), dynamic_slice_sizes={1} | dynamic-slice | bytes 12
  33.6 0.2 dynamic-update-slice
  33.9 12.5 %all-reduce = f32[64]{0:T(128)S(1)} all-reduce(f32[64]{0:T(128)S(1)} %dynamic-update-slice), channel_id=2, replica_groups=mesh['seq'=8,'head'=4] {'seq'}, use_global_device_ids=true, to_apply=%add | all-reduce | flops 64 | bytes 512
  46.4 0.1 reshape.236
  46.5 1.6 %copy.93 = bf16[2,4,8,1024]{3,2,0,1:T(8,128)(2,1)} copy(bf16[2,4,8,1024]{3,2,1,0:T(8,128)(2,1)} %bitcast.145) | data formatting | bytes 262144 | tf_op jit(solution)/shard_map/all_to_all | solution.py:81
  48.1 0.0 all-to-all-done.2
  48.1 4.8 %all-to-all-start.1 = ((bf16[16,4,1024]{2,0,1:T(8,128)(2,1)}), bf16[16,4,1024]{2,0,1:T(8,128)(2,1)S(1)}, u32[]{:S(2)}, u32[]{:S(2)}) async-start(bf16[16,4,1024]{2,0,1:T(8,128)(2,1)} %bitcast.137), calls=%async_computation.1 | async-start | bytes 262144 | tf_op jit(solution)/shard_map/all_to_all | solution.py:81
  52.8 0.7 fusion.25
  53.6 9.1 %all_gather.19 = bf16[512,128]{1,0:T(8,128)(2,1)S(1)} all-gather(bf16[64,128]{1,0:T(8,128)(2,1)S(1)} %bitcast.148), channel_id=1, replica_groups=mesh['seq'=8,'head'=4] {'seq'}, dimensions={0}, use_global_device_ids=true | all-gather | bytes 147456 | tf_op jit(solution)/shard_map/all_gather | solution.py:97
  62.7 8.4 %all_gather.20 = bf16[512,128]{1,0:T(8,128)(2,1)S(1)} all-gather(bf16[64,128]{1,0:T(8,128)(2,1)S(1)} %bitcast.149), channel_id=1, replica_groups=mesh['seq'=8,'head'=4] {'seq'}, dimensions={0}, use_global_device_ids=true | all-gather | bytes 147456 | tf_op jit(solution)/shard_map/all_gather | solution.py:98
  71.0 0.0 all-to-all-done.1
  71.1 0.4 select_reduce_fusion
  71.4 0.4 fusion.7
  71.8 0.1 copy.42
  71.9 0.1 copy.45
  72.0 0.5 fusion.6
  72.5 0.0 copy-start.1
  72.5 0.7 copy.92
  73.1 0.6 fusion.33
  73.8 0.0 all-gather.4.cloned.1.call-done
  73.8 9.7 %while.9 = (s32[]{:T(128)}, f32[8,128,128]{2,1,0:T(8,128)S(1)}, s32[]{:T(128)}, f32[8,8]{1,0:T(8,128)S(1)}, f32[8,8,128,128]{3,2,1,0:T(8,128)}, /*index=5*/s32[]{:T(128)}, s32[]{:T(128)}) while((s32[]{:T(128)}, f32[8,128,128]{2,1,0:T(8,128)S(1)}, s32[]{:T(128)}, f32[8,8]{1,0:T(8,128)S(1)}, f32[8,8,128,128]{3,2,1,0:T(8,128)}, ...), condition=%wide.region_2.3_spmd.clone, body=%wide.region_1.2_spmd.clone.sunk | while | flops 524292 | bytes 1573065 | solution.py:25
  73.8 1.2 %fusion.49 = f32[8,128,128]{2,1,0:T(8,128)S(1)} fusion(f32[8,8,128,128]{3,2,1,0:T(8,128)} %get-tuple-element.216, s32[]{:T(128)} %get-tuple-element.205, f32[8,128,128]{2,1,0:T(8,128)S(1)} %get-tuple-element.206, f32[8]{0:T(128)S(1)} %dynamic-slice_bitcast_fusion.2, pred[]{:T(512)S(6)} %compare.3, pred[]{:T(512)S(6)} %lt.33), kind=kLoop, calls=%fused_computation.1.clone.1 | loop fusion | flops 524288 | bytes 1572902 | tf_op jit(solution)/shard_map/while/body/eval_jaxpr/jit(_where)/select_n | solution.py:23
  75.0 1.2 %fusion.49 = f32[8,128,128]{2,1,0:T(8,128)S(1)} fusion(f32[8,8,128,128]{3,2,1,0:T(8,128)} %get-tuple-element.216, s32[]{:T(128)} %get-tuple-element.205, f32[8,128,128]{2,1,0:T(8,128)S(1)} %get-tuple-element.206, f32[8]{0:T(128)S(1)} %dynamic-slice_bitcast_fusion.2, pred[]{:T(512)S(6)} %compare.3, pred[]{:T(512)S(6)} %lt.33), kind=kLoop, calls=%fused_computation.1.clone.1 | loop fusion | flops 524288 | bytes 1572902 | tf_op jit(solution)/shard_map/while/body/eval_jaxpr/jit(_where)/select_n | solution.py:23
  76.2 1.2 %fusion.49 = f32[8,128,128]{2,1,0:T(8,128)S(1)} fusion(f32[8,8,128,128]{3,2,1,0:T(8,128)} %get-tuple-element.216, s32[]{:T(128)} %get-tuple-element.205, f32[8,128,128]{2,1,0:T(8,128)S(1)} %get-tuple-element.206, f32[8]{0:T(128)S(1)} %dynamic-slice_bitcast_fusion.2, pred[]{:T(512)S(6)} %compare.3, pred[]{:T(512)S(6)} %lt.33), kind=kLoop, calls=%fused_computation.1.clone.1 | loop fusion | flops 524288 | bytes 1572902 | tf_op jit(solution)/shard_map/while/body/eval_jaxpr/jit(_where)/select_n | solution.py:23
  77.4 1.2 %fusion.49 = f32[8,128,128]{2,1,0:T(8,128)S(1)} fusion(f32[8,8,128,128]{3,2,1,0:T(8,128)} %get-tuple-element.216, s32[]{:T(128)} %get-tuple-element.205, f32[8,128,128]{2,1,0:T(8,128)S(1)} %get-tuple-element.206, f32[8]{0:T(128)S(1)} %dynamic-slice_bitcast_fusion.2, pred[]{:T(512)S(6)} %compare.3, pred[]{:T(512)S(6)} %lt.33), kind=kLoop, calls=%fused_computation.1.clone.1 | loop fusion | flops 524288 | bytes 1572902 | tf_op jit(solution)/shard_map/while/body/eval_jaxpr/jit(_where)/select_n | solution.py:23
  78.6 1.2 %fusion.49 = f32[8,128,128]{2,1,0:T(8,128)S(1)} fusion(f32[8,8,128,128]{3,2,1,0:T(8,128)} %get-tuple-element.216, s32[]{:T(128)} %get-tuple-element.205, f32[8,128,128]{2,1,0:T(8,128)S(1)} %get-tuple-element.206, f32[8]{0:T(128)S(1)} %dynamic-slice_bitcast_fusion.2, pred[]{:T(512)S(6)} %compare.3, pred[]{:T(512)S(6)} %lt.33), kind=kLoop, calls=%fused_computation.1.clone.1 | loop fusion | flops 524288 | bytes 1572902 | tf_op jit(solution)/shard_map/while/body/eval_jaxpr/jit(_where)/select_n | solution.py:23
  79.8 1.2 %fusion.49 = f32[8,128,128]{2,1,0:T(8,128)S(1)} fusion(f32[8,8,128,128]{3,2,1,0:T(8,128)} %get-tuple-element.216, s32[]{:T(128)} %get-tuple-element.205, f32[8,128,128]{2,1,0:T(8,128)S(1)} %get-tuple-element.206, f32[8]{0:T(128)S(1)} %dynamic-slice_bitcast_fusion.2, pred[]{:T(512)S(6)} %compare.3, pred[]{:T(512)S(6)} %lt.33), kind=kLoop, calls=%fused_computation.1.clone.1 | loop fusion | flops 524288 | bytes 1572902 | tf_op jit(solution)/shard_map/while/body/eval_jaxpr/jit(_where)/select_n | solution.py:23
  81.0 1.2 %fusion.49 = f32[8,128,128]{2,1,0:T(8,128)S(1)} fusion(f32[8,8,128,128]{3,2,1,0:T(8,128)} %get-tuple-element.216, s32[]{:T(128)} %get-tuple-element.205, f32[8,128,128]{2,1,0:T(8,128)S(1)} %get-tuple-element.206, f32[8]{0:T(128)S(1)} %dynamic-slice_bitcast_fusion.2, pred[]{:T(512)S(6)} %compare.3, pred[]{:T(512)S(6)} %lt.33), kind=kLoop, calls=%fused_computation.1.clone.1 | loop fusion | flops 524288 | bytes 1572902 | tf_op jit(solution)/shard_map/while/body/eval_jaxpr/jit(_where)/select_n | solution.py:23
  82.2 1.2 %fusion.49 = f32[8,128,128]{2,1,0:T(8,128)S(1)} fusion(f32[8,8,128,128]{3,2,1,0:T(8,128)} %get-tuple-element.216, s32[]{:T(128)} %get-tuple-element.205, f32[8,128,128]{2,1,0:T(8,128)S(1)} %get-tuple-element.206, f32[8]{0:T(128)S(1)} %dynamic-slice_bitcast_fusion.2, pred[]{:T(512)S(6)} %compare.3, pred[]{:T(512)S(6)} %lt.33), kind=kLoop, calls=%fused_computation.1.clone.1 | loop fusion | flops 524288 | bytes 1572902 | tf_op jit(solution)/shard_map/while/body/eval_jaxpr/jit(_where)/select_n | solution.py:23
  83.4 0.0 copy-done.1
  83.4 0.4 fusion.2
  83.8 0.4 multiply_reduce_fusion
  84.2 0.8 copy_bitcast_fusion.1
  (15 shorter events, 0.1 us)
Async XLA Ops:
  7.2 4.4 %copy-start = (bf16[64,1024]{1,0:T(8,128)(2,1)S(1)}, bf16[64,1024]{1,0:T(8,128)(2,1)}, u32[]{:S(2)}) copy-start(bf16[64,1024]{1,0:T(8,128)(2,1)} %param.12) | copy-start | bytes 393220
  7.2 66.6 %all-gather.4.cloned.1.call-start = ((), (), s32[]{:S(2)}) async-start(), calls=%async_computation.3 | async-start | bytes 4718592 | tf_op jit(solution)/shard_map/all_gather | solution.py:13
  15.3 11.9 %all-to-all-start = ((bf16[16,4,128]{2,0,1:T(8,128)(2,1)}), bf16[16,4,128]{2,0,1:T(8,128)(2,1)S(1)}, u32[]{:S(2)}, u32[]{:S(2)}) async-start(bf16[16,4,128]{2,0,1:T(8,128)(2,1)} %copy_bitcast_fusion.4), calls=%async_computation | async-start | bytes 32768 | tf_op jit(solution)/shard_map/all_to_all | solution.py:82
  27.3 20.8 %all-to-all-start.2 = ((bf16[16,4,128]{2,0,1:T(8,128)(2,1)}), bf16[16,4,128]{2,0,1:T(8,128)(2,1)S(1)}, u32[]{:S(2)}, u32[]{:S(2)}) async-start(bf16[16,4,128]{2,0,1:T(8,128)(2,1)} %copy_bitcast_fusion.3), calls=%async_computation.2 | async-start | bytes 32768 | tf_op jit(solution)/shard_map/all_to_all | solution.py:83
  48.1 23.0 %all-to-all-start.1 = ((bf16[16,4,1024]{2,0,1:T(8,128)(2,1)}), bf16[16,4,1024]{2,0,1:T(8,128)(2,1)S(1)}, u32[]{:S(2)}, u32[]{:S(2)}) async-start(bf16[16,4,1024]{2,0,1:T(8,128)(2,1)} %bitcast.137), calls=%async_computation.1 | async-start | bytes 262144 | tf_op jit(solution)/shard_map/all_to_all | solution.py:81
  72.5 11.0 %copy-start.1 = (bf16[64,1024]{1,0:T(8,128)(2,1)S(1)}, bf16[64,1024]{1,0:T(8,128)(2,1)}, u32[]{:S(2)}) copy-start(bf16[64,1024]{1,0:T(8,128)(2,1)} %param.10) | copy-start | bytes 393220
Sparse Core Ops, SparseCore 0:
  14.1 39.5 all-gather.3
where the time goes:
time: 92.9 us; the launch traced here: 91.8 us
  blocking collectives  30 us (32%)
  between operations  15.5 us (17%)
  other arithmetic  15.1 us (16%)
  starting transfers between devices  14.4 us (16%)
  local copies, waits for them, and re-layouts  7.97 us (9%)
  matrix products  5.12 us (6%)
  waiting for transfers between devices  3.56 us (4%)
    unnamed x1, blocking collectives  12.5 us
    select_n x8, other arithmetic, lap(): return jax.tree.map(lambda a, b: jnp.where(reached, a, b), new, before)  9.38 us
    all_gather x1, blocking collectives, softmax_part(): key_piece = lax.all_gather(keys_local, 'seq', axis=0, tiled=True)  9.07 us
    all_gather x1, blocking collectives, softmax_part(): value_piece = lax.all_gather(values_local, 'seq', axis=0, tiled=True)  8.36 us
    all_to_all x1, starting transfers between devices, softmax_part(): lax.all_to_all(key_soft, 'head', split_axis=1, concat_axis=0, tiled=True)  6.32 us
    all_to_all x1, starting transfers between devices, softmax_part(): lax.all_to_all(query_soft, 'head', split_axis=1, concat_axis=0, tiled=True)  4.78 us
    all_to_all x1, waiting for transfers between devices, softmax_part(): lax.all_to_all(key_soft, 'head', split_axis=1, concat_axis=0, tiled=True)  3.54 us
    all_to_all x1, starting transfers between devices, softmax_part(): lax.all_to_all(value_soft, 'head', split_axis=1, concat_axis=0, tiled=True)  3.25 us
  transfers between devices with their start and end apart: 4, of which 1 were waited for; matrix products, arithmetic and copies ran while one was open for 12% of the time, Pallas kernels for 0%

commit v1 on v0

--- a/solution.py
+++ b/solution.py
@@ -94,8 +94,13 @@
         jnp.zeros((span_len, kv_count, group_size), jnp.float32),
         jnp.zeros((span_len, kv_count, group_size, DH), jnp.float32),
     )
-    key_piece = lax.all_gather(keys_local, "seq", axis=0, tiled=True)
-    value_piece = lax.all_gather(values_local, "seq", axis=0, tiled=True)
+    key_piece, value_piece = jnp.split(
+        lax.all_gather(
+            jnp.concatenate([keys_local, values_local], axis=1), "seq", axis=0, tiled=True
+        ),
+        [keys_local.shape[1]],
+        axis=1,
+    )
     piece_rows = key_piece.shape[0]
     block_rows = max(
         (divisor for divisor in range(1, min(piece_rows, 1024) + 1) if piece_rows % divisor == 0)

time: 92.9 us -> 85.5 us (0.920)
  blocking collectives: 30 us -> 21.3 us
  waiting for transfers between devices: 3.56 us -> 6.39 us
  starting transfers between devices: 14.4 us -> 13 us
    all_gather x2 -> x1, blocking collectives: 17.4 us -> 9.31 us  [softmax_part(): lax.all_gather(jnp.concatenate([keys_local, values_local], axis=1), 'seq'...]
    all_to_all x1, waiting for transfers between devices: 0.01 us -> 3.54 us  [softmax_part(): lax.all_to_all(value_soft, 'head', split_axis=1, concat_axis=0, tiled=True)]
    all_to_all x1, starting transfers between devices: 6.32 us -> 3.25 us  [softmax_part(): lax.all_to_all(key_soft, 'head', split_axis=1, concat_axis=0, tiled=True)]
    all_to_all x1, starting transfers between devices: 3.25 us -> 6.32 us  [softmax_part(): lax.all_to_all(value_soft, 'head', split_axis=1, concat_axis=0, tiled=True)]
    all_to_all x1, starting transfers between devices: 4.78 us -> 3.34 us  [softmax_part(): lax.all_to_all(query_soft, 'head', split_axis=1, concat_axis=0, tiled=True)]
  transfers between devices with their start and end apart: 4 -> 4, of which waited for: 1 -> 2; matrix products, arithmetic and copies ran while one was open for 12% -> 13% of each run, Pallas kernels for 0% -> 0%
where the time goes in v1:
time: 85.5 us; the launch traced here: 84.5 us
  blocking collectives  21.3 us (25%)
  between operations  15.5 us (18%)
  other arithmetic  15.1 us (18%)
  starting transfers between devices  13 us (15%)
  local copies, waits for them, and re-layouts  7.89 us (9%)
  waiting for transfers between devices  6.39 us (7%)
  matrix products  5.03 us (6%)
    unnamed x1, blocking collectives  12 us
    select_n x8, other arithmetic, lap(): return jax.tree.map(lambda a, b: jnp.where(reached, a, b), new, before)  9.38 us
    all_gather x1, blocking collectives, softmax_part(): lax.all_gather(jnp.concatenate([keys_local, values_local], axis=1), 'seq'...  9.31 us
    all_to_all x1, starting transfers between devices, softmax_part(): lax.all_to_all(value_soft, 'head', split_axis=1, concat_axis=0, tiled=True)  6.32 us
    all_to_all x1, waiting for transfers between devices, softmax_part(): lax.all_to_all(value_soft, 'head', split_axis=1, concat_axis=0, tiled=True)  3.54 us
    all_to_all x1, starting transfers between devices, softmax_part(): lax.all_to_all(query_soft, 'head', split_axis=1, concat_axis=0, tiled=True)  3.34 us
    all_to_all x1, starting transfers between devices, softmax_part(): lax.all_to_all(key_soft, 'head', split_axis=1, concat_axis=0, tiled=True)  3.25 us
    all_to_all x1, waiting for transfers between devices, softmax_part(): lax.all_to_all(key_soft, 'head', split_axis=1, concat_axis=0, tiled=True)  2.83 us
  transfers between devices with their start and end apart: 4, of which 2 were waited for; matrix products, arithmetic and copies ran while one was open for 13% of the time, Pallas kernels for 0%

profile of v1, /device:TPU:0, one launch (start us, length us, event | category | flops | bytes accessed | tf_op | source)
XLA Modules:
  0.0 84.5 jit_solution(9442633476704783729)
XLA Ops:
  7.2 0.0 copy-start
  7.2 0.0 all-gather.4.cloned.1.call-start
  7.2 1.2 %slice.8 = s32[1]{0:T(128)} slice(s32[64]{0:T(128)} %param.17), slice={[63:64]} | slice | bytes 8 | tf_op jit(solution)/shard_map/slice | solution.py:46
  9.1 1.3 %compare_convert_fusion = (f32[64]{0:T(128)S(1)}, f32[64]{0:T(128)S(1)}) fusion(s32[64]{0:T(128)} %param.17, s32[]{:T(128)S(6)} %mul.138, s32[]{:T(128)} %bitcast.1), kind=kLoop, calls=%fused_computation.68 | loop fusion | flops 256 | bytes 776 | tf_op jit(solution)/shard_map/convert_element_type | solution.py:48
  10.4 0.9 %reduce_window_sum.11 = f32[8,64]{1,0:T(8,128)S(1)} reduce-window(f32[8,64]{1,0:T(8,128)} %param.13, f32[]{:T(128)} %constant.60.clone.1), window={size=1x64 pad=0_0x63_0}, to_apply=%region_0.0 | reduce-window | flops 32256 | bytes 4100 | tf_op jit(solution)/shard_map/jit(cumsum)/reduce_window_sum | solution.py:30
  11.3 0.2 slice_reduce_fusion
  11.5 0.1 multiply_bitcast_fusion
  11.6 0.0 copy-done
  11.6 2.4 %fusion.15 = f32[8,128,128]{2,1,0:T(8,128)} fusion(f32[64,8]{0,1:T(8,128)S(1)} %get-tuple-element.158, bf16[64,1024]{1,0:T(8,128)(2,1)S(1)} %copy-done, bf16[64,1024]{1,0:T(8,128)(2,1)} %param.11), kind=kOutput, calls=%fused_computation.25 | convolution fusion | flops 100794368 | bytes 788480 | tf_op jit(solution)/shard_map/shd,she->hde/dot_general | solution.py:45
  14.0 0.0 all-gather.4.cloned.1.call-update
  14.0 1.3 %copy_bitcast_fusion.3 = bf16[16,4,128]{2,0,1:T(8,128)(2,1)} fusion(bf16[16,512]{1,0:T(8,128)(2,1)} %param.16), kind=kLoop, calls=%fused_computation.53 | loop fusion | bytes 32768 | tf_op jit(solution)/shard_map/all_to_all | solution.py:83
  15.3 6.3 %all-to-all-start.1 = ((bf16[16,4,128]{2,0,1:T(8,128)(2,1)}), bf16[16,4,128]{2,0,1:T(8,128)(2,1)S(1)}, u32[]{:S(2)}, u32[]{:S(2)}) async-start(bf16[16,4,128]{2,0,1:T(8,128)(2,1)} %copy_bitcast_fusion.3), calls=%async_computation.1 | async-start | bytes 32768 | tf_op jit(solution)/shard_map/all_to_all | solution.py:83
  21.7 1.3 %copy_bitcast_fusion.4 = bf16[16,4,128]{2,0,1:T(8,128)(2,1)} fusion(bf16[16,512]{1,0:T(8,128)(2,1)} %param.15), kind=kLoop, calls=%fused_computation.54 | loop fusion | bytes 32768 | tf_op jit(solution)/shard_map/all_to_all | solution.py:82
  23.0 0.7 compare_and_fusion
  23.7 3.5 %all-to-all-done.1 = bf16[16,4,128]{2,0,1:T(8,128)(2,1)S(1)} async-done(((bf16[16,4,128]{2,0,1:T(8,128)(2,1)}), bf16[16,4,128]{2,0,1:T(8,128)(2,1)S(1)}, u32[]{:S(2)}, u32[]{:S(2)}) %all-to-all-start.1) | async-done | bytes 16416 | tf_op jit(solution)/shard_map/all_to_all | solution.py:83
  27.3 3.3 %all-to-all-start = ((bf16[16,4,128]{2,0,1:T(8,128)(2,1)}), bf16[16,4,128]{2,0,1:T(8,128)(2,1)S(1)}, u32[]{:S(2)}, u32[]{:S(2)}) async-start(bf16[16,4,128]{2,0,1:T(8,128)(2,1)} %copy_bitcast_fusion.4), calls=%async_computation | async-start | bytes 32768 | tf_op jit(solution)/shard_map/all_to_all | solution.py:82
  30.5 1.2 %convolution_multiply_fusion.1 = f32[8,64,64]{2,1,0:T(8,128)S(1)} fusion(f32[8,64]{1,0:T(8,128)S(1)} %reduce_window_sum.11, pred[64,64]{1,0:T(8,128)(4,1)S(1)} %compare_and_fusion, bf16[64,1024]{1,0:T(8,128)(2,1)} %param.11, bf16[64,1024]{1,0:T(8,128)(2,1)} %param.10), kind=kOutput, calls=%fused_computation.11 | convolution fusion | flops 8519680 | bytes 399360 | tf_op jit(solution)/shard_map/thd,shd->hts/dot_general | solution.py:38
  31.7 1.6 %copy.84 = bf16[2,4,8,1024]{3,2,0,1:T(8,128)(2,1)} copy(bf16[2,4,8,1024]{3,2,1,0:T(8,128)(2,1)} %bitcast.148) | data formatting | bytes 262144 | tf_op jit(solution)/shard_map/all_to_all | solution.py:81
  33.3 2.8 %all-to-all-done = bf16[16,4,128]{2,0,1:T(8,128)(2,1)S(1)} async-done(((bf16[16,4,128]{2,0,1:T(8,128)(2,1)}), bf16[16,4,128]{2,0,1:T(8,128)(2,1)S(1)}, u32[]{:S(2)}, u32[]{:S(2)}) %all-to-all-start) | async-done | bytes 16416 | tf_op jit(solution)/shard_map/all_to_all | solution.py:82
  36.1 3.3 %all-to-all-start.2 = ((bf16[16,4,1024]{2,0,1:T(8,128)(2,1)}), bf16[16,4,1024]{2,0,1:T(8,128)(2,1)S(1)}, u32[]{:S(2)}, u32[]{:S(2)}) async-start(bf16[16,4,1024]{2,0,1:T(8,128)(2,1)} %bitcast.139), calls=%async_computation.2 | async-start | bytes 262144 | tf_op jit(solution)/shard_map/all_to_all | solution.py:81
  39.5 0.8 fusion.27
  40.2 1.2 %dynamic-slice = u32[1]{0:T(128)} dynamic-slice(u32[32]{0:T(128)} %constant.72, u32[]{:T(128)S(6)} %add.102), dynamic_slice_sizes={1} | dynamic-slice | bytes 12
  42.1 0.2 dynamic-update-slice
  42.4 12.0 %all-reduce = f32[64]{0:T(128)S(1)} all-reduce(f32[64]{0:T(128)S(1)} %dynamic-update-slice), channel_id=2, replica_groups=mesh['seq'=8,'head'=4] {'seq'}, use_global_device_ids=true, to_apply=%add | all-reduce | flops 64 | bytes 512
  54.4 0.1 reshape.236
  54.5 9.3 %all_gather.16 = bf16[512,256]{1,0:T(8,128)(2,1)S(1)} all-gather(bf16[64,256]{1,0:T(8,128)(2,1)S(1)} %pad_maximum_fusion), channel_id=1, replica_groups=mesh['seq'=8,'head'=4] {'seq'}, dimensions={0}, use_global_device_ids=true | all-gather | bytes 294912 | tf_op jit(solution)/shard_map/all_gather | solution.py:98
  63.8 0.0 all-to-all-done.2
  63.8 0.4 select_reduce_fusion
  64.2 0.4 fusion.8
  64.6 0.4 fusion.7
  65.0 0.1 copy.38
  65.1 0.0 copy-start.1
  65.1 0.7 copy.83
  65.8 0.6 fusion.35
  66.4 0.0 all-gather.4.cloned.1.call-done
  66.4 9.7 %while.9 = (s32[]{:T(128)}, f32[8,128,128]{2,1,0:T(8,128)S(1)}, s32[]{:T(128)}, f32[8,8]{1,0:T(8,128)S(1)}, f32[8,8,128,128]{3,2,1,0:T(8,128)}, /*index=5*/s32[]{:T(128)}, s32[]{:T(128)}) while((s32[]{:T(128)}, f32[8,128,128]{2,1,0:T(8,128)S(1)}, s32[]{:T(128)}, f32[8,8]{1,0:T(8,128)S(1)}, f32[8,8,128,128]{3,2,1,0:T(8,128)}, ...), condition=%wide.region_2.3_spmd.clone, body=%wide.region_1.2_spmd.clone.sunk | while | flops 524292 | bytes 1573073 | solution.py:25
  66.4 1.2 %fusion.52 = f32[8,128,128]{2,1,0:T(8,128)S(1)} fusion(f32[8,8,128,128]{3,2,1,0:T(8,128)} %get-tuple-element.214, s32[]{:T(128)S(6)} %copy.88, f32[8,128,128]{2,1,0:T(8,128)S(1)} %get-tuple-element.204, f32[8]{0:T(128)S(1)} %dynamic-slice_bitcast_fusion.2, pred[]{:T(512)S(6)} %compare.3, pred[]{:T(512)S(6)} %lt.33), kind=kLoop, calls=%fused_computation.1.clone.1 | loop fusion | flops 524288 | bytes 1572902 | tf_op jit(solution)/shard_map/while/body/eval_jaxpr/jit(_where)/select_n | solution.py:23
  67.6 1.2 %fusion.52 = f32[8,128,128]{2,1,0:T(8,128)S(1)} fusion(f32[8,8,128,128]{3,2,1,0:T(8,128)} %get-tuple-element.214, s32[]{:T(128)S(6)} %copy.88, f32[8,128,128]{2,1,0:T(8,128)S(1)} %get-tuple-element.204, f32[8]{0:T(128)S(1)} %dynamic-slice_bitcast_fusion.2, pred[]{:T(512)S(6)} %compare.3, pred[]{:T(512)S(6)} %lt.33), kind=kLoop, calls=%fused_computation.1.clone.1 | loop fusion | flops 524288 | bytes 1572902 | tf_op jit(solution)/shard_map/while/body/eval_jaxpr/jit(_where)/select_n | solution.py:23
  68.8 1.2 %fusion.52 = f32[8,128,128]{2,1,0:T(8,128)S(1)} fusion(f32[8,8,128,128]{3,2,1,0:T(8,128)} %get-tuple-element.214, s32[]{:T(128)S(6)} %copy.88, f32[8,128,128]{2,1,0:T(8,128)S(1)} %get-tuple-element.204, f32[8]{0:T(128)S(1)} %dynamic-slice_bitcast_fusion.2, pred[]{:T(512)S(6)} %compare.3, pred[]{:T(512)S(6)} %lt.33), kind=kLoop, calls=%fused_computation.1.clone.1 | loop fusion | flops 524288 | bytes 1572902 | tf_op jit(solution)/shard_map/while/body/eval_jaxpr/jit(_where)/select_n | solution.py:23
  70.0 1.2 %fusion.52 = f32[8,128,128]{2,1,0:T(8,128)S(1)} fusion(f32[8,8,128,128]{3,2,1,0:T(8,128)} %get-tuple-element.214, s32[]{:T(128)S(6)} %copy.88, f32[8,128,128]{2,1,0:T(8,128)S(1)} %get-tuple-element.204, f32[8]{0:T(128)S(1)} %dynamic-slice_bitcast_fusion.2, pred[]{:T(512)S(6)} %compare.3, pred[]{:T(512)S(6)} %lt.33), kind=kLoop, calls=%fused_computation.1.clone.1 | loop fusion | flops 524288 | bytes 1572902 | tf_op jit(solution)/shard_map/while/body/eval_jaxpr/jit(_where)/select_n | solution.py:23
  71.2 1.2 %fusion.52 = f32[8,128,128]{2,1,0:T(8,128)S(1)} fusion(f32[8,8,128,128]{3,2,1,0:T(8,128)} %get-tuple-element.214, s32[]{:T(128)S(6)} %copy.88, f32[8,128,128]{2,1,0:T(8,128)S(1)} %get-tuple-element.204, f32[8]{0:T(128)S(1)} %dynamic-slice_bitcast_fusion.2, pred[]{:T(512)S(6)} %compare.3, pred[]{:T(512)S(6)} %lt.33), kind=kLoop, calls=%fused_computation.1.clone.1 | loop fusion | flops 524288 | bytes 1572902 | tf_op jit(solution)/shard_map/while/body/eval_jaxpr/jit(_where)/select_n | solution.py:23
  72.5 1.2 %fusion.52 = f32[8,128,128]{2,1,0:T(8,128)S(1)} fusion(f32[8,8,128,128]{3,2,1,0:T(8,128)} %get-tuple-element.214, s32[]{:T(128)S(6)} %copy.88, f32[8,128,128]{2,1,0:T(8,128)S(1)} %get-tuple-element.204, f32[8]{0:T(128)S(1)} %dynamic-slice_bitcast_fusion.2, pred[]{:T(512)S(6)} %compare.3, pred[]{:T(512)S(6)} %lt.33), kind=kLoop, calls=%fused_computation.1.clone.1 | loop fusion | flops 524288 | bytes 1572902 | tf_op jit(solution)/shard_map/while/body/eval_jaxpr/jit(_where)/select_n | solution.py:23
  73.7 1.2 %fusion.52 = f32[8,128,128]{2,1,0:T(8,128)S(1)} fusion(f32[8,8,128,128]{3,2,1,0:T(8,128)} %get-tuple-element.214, s32[]{:T(128)S(6)} %copy.88, f32[8,128,128]{2,1,0:T(8,128)S(1)} %get-tuple-element.204, f32[8]{0:T(128)S(1)} %dynamic-slice_bitcast_fusion.2, pred[]{:T(512)S(6)} %compare.3, pred[]{:T(512)S(6)} %lt.33), kind=kLoop, calls=%fused_computation.1.clone.1 | loop fusion | flops 524288 | bytes 1572902 | tf_op jit(solution)/shard_map/while/body/eval_jaxpr/jit(_where)/select_n | solution.py:23
  74.9 1.2 %fusion.52 = f32[8,128,128]{2,1,0:T(8,128)S(1)} fusion(f32[8,8,128,128]{3,2,1,0:T(8,128)} %get-tuple-element.214, s32[]{:T(128)S(6)} %copy.88, f32[8,128,128]{2,1,0:T(8,128)S(1)} %get-tuple-element.204, f32[8]{0:T(128)S(1)} %dynamic-slice_bitcast_fusion.2, pred[]{:T(512)S(6)} %compare.3, pred[]{:T(512)S(6)} %lt.33), kind=kLoop, calls=%fused_computation.1.clone.1 | loop fusion | flops 524288 | bytes 1572902 | tf_op jit(solution)/shard_map/while/body/eval_jaxpr/jit(_where)/select_n | solution.py:23
  76.1 0.0 copy-done.1
  76.1 0.4 fusion.3
  76.5 0.4 multiply_reduce_fusion
  76.8 0.8 copy_bitcast_fusion.1
  (16 shorter events, 0.1 us)
Async XLA Ops:
  7.2 4.4 %copy-start = (bf16[64,1024]{1,0:T(8,128)(2,1)S(1)}, bf16[64,1024]{1,0:T(8,128)(2,1)}, u32[]{:S(2)}) copy-start(bf16[64,1024]{1,0:T(8,128)(2,1)} %param.12) | copy-start | bytes 393220
  7.2 59.2 %all-gather.4.cloned.1.call-start = ((), (), s32[]{:S(2)}) async-start(), calls=%async_computation.3 | async-start | bytes 4718592 | tf_op jit(solution)/shard_map/all_gather | solution.py:13
  15.3 11.9 %all-to-all-start.1 = ((bf16[16,4,128]{2,0,1:T(8,128)(2,1)}), bf16[16,4,128]{2,0,1:T(8,128)(2,1)S(1)}, u32[]{:S(2)}, u32[]{:S(2)}) async-start(bf16[16,4,128]{2,0,1:T(8,128)(2,1)} %copy_bitcast_fusion.3), calls=%async_computation.1 | async-start | bytes 32768 | tf_op jit(solution)/shard_map/all_to_all | solution.py:83
  27.3 8.8 %all-to-all-start = ((bf16[16,4,128]{2,0,1:T(8,128)(2,1)}), bf16[16,4,128]{2,0,1:T(8,128)(2,1)S(1)}, u32[]{:S(2)}, u32[]{:S(2)}) async-start(bf16[16,4,128]{2,0,1:T(8,128)(2,1)} %copy_bitcast_fusion.4), calls=%async_computation | async-start | bytes 32768 | tf_op jit(solution)/shard_map/all_to_all | solution.py:82
  36.1 27.7 %all-to-all-start.2 = ((bf16[16,4,1024]{2,0,1:T(8,128)(2,1)}), bf16[16,4,1024]{2,0,1:T(8,128)(2,1)S(1)}, u32[]{:S(2)}, u32[]{:S(2)}) async-start(bf16[16,4,1024]{2,0,1:T(8,128)(2,1)} %bitcast.139), calls=%async_computation.2 | async-start | bytes 262144 | tf_op jit(solution)/shard_map/all_to_all | solution.py:81
  65.1 11.0 %copy-start.1 = (bf16[64,1024]{1,0:T(8,128)(2,1)S(1)}, bf16[64,1024]{1,0:T(8,128)(2,1)}, u32[]{:S(2)}) copy-start(bf16[64,1024]{1,0:T(8,128)(2,1)} %param.10) | copy-start | bytes 393220
Sparse Core Ops, SparseCore 0:
  14.1 39.4 all-gather.3
